TPU v7x, 32 devices: a whole 2x2x4 slice. The times are simulated.
32 devices in a mesh: dp: 2 (over x), tensor: 8 (over z, y), pipe: 2 (over core).
Axes of the slice: x: 2, y: 2, z: 4, core: 2. Of those that a mesh axis runs over, the one named last changes fastest.
Arguments:
- hidden: bfloat16 [2, 1024, 7168], P('pipe', ('dp', 'tensor')), may hold values from -200 to 200
- head_table: bfloat16 [81920, 7168], P(('dp', 'tensor')), may hold values from -1 to 1
- targets: int32 [2, 1024], P('pipe', ('dp', 'tensor')), may hold values from 0 to 81919
Outputs:
- token_loss: float32 [2, 1024], P('pipe', ('dp', 'tensor'))
- mean_loss: float32 [], replicated
All inputs are finite; a program needn't handle non-finite values.
Results may differ from a plain program's by a relative error of at most 0.0003.
Values may be sent and summed in bfloat16 or wider, within the bound.
No kernel may reach another device: no remote copies, remote signals or barrier semaphores. Data moves between devices by JAX's collectives and lax.ppermute only.
A program may use at most 192 MiB of HBM per device.

v0:
```python
import jax
import jax.numpy as jnp
from jax import lax
from jax.sharding import PartitionSpec as P


def body(hidden, head_table, targets):
    row_count = head_table.shape[0]
    position = lax.axis_index(("dp", "tensor"))
    offset = position * row_count
    tokens_own = hidden[0]
    labels_own = targets[0]
    own_count = tokens_own.shape[0]
    columns = lax.broadcasted_iota(jnp.int32, (1, row_count), 1)
    gathered, labels = (
        lax.all_gather(tokens_own, ("dp", "tensor"), axis=0, tiled=True),
        lax.all_gather(labels_own, ("dp", "tensor"), axis=0, tiled=True),
    )
    logits = lax.dot_general(
        gathered, head_table, (((1,), (1,)), ((), ())), preferred_element_type=jnp.float32
    )
    local_ids = (labels - offset)[:, None]
    picked = jnp.sum(jnp.where(columns == local_ids, logits, 0.0), axis=1)
    logits, picked = (logits, picked)
    local_maxima = jnp.max(logits, axis=1)
    maxima = lax.pmax(local_maxima, ("dp", "tensor"))
    exp_sums = jnp.sum(jnp.exp(logits - maxima[:, None]), axis=1)
    totals, chosen = lax.psum((exp_sums, picked), ("dp", "tensor"))
    losses = maxima + jnp.log(totals) - chosen
    own_losses = lax.dynamic_slice_in_dim(losses, position * own_count, own_count, 0)
    loss_sum = lax.psum(jnp.sum(losses), "pipe")
    mean_loss = loss_sum / (losses.shape[0] * lax.axis_size("pipe"))
    return (own_losses[None, :], mean_loss)


def solution(mesh):
    in_specs = (
        P("pipe", ("dp", "tensor"), None),
        P(("dp", "tensor"), None),
        P("pipe", ("dp", "tensor")),
    )
    out_specs = (P("pipe", ("dp", "tensor")), P())
    return jax.shard_map(body, mesh=mesh, in_specs=in_specs, out_specs=out_specs, check_vma=False)
```

profile of v0, /device:TPU:0, one launch (start us, length us, event | category | flops | bytes accessed | tf_op | source)
XLA Modules:
  0.0 370.6 jit_solution(1653511090591210883)
XLA Ops:
  7.2 0.0 all-gather.4.cloned.1.call-start
  7.2 0.7 all-gather.4.cloned.1.call-update
  7.9 1.2 dynamic-slice
  9.8 0.8 bitcast_dynamic-update-slice_fusion
  10.6 16.3 %all-reduce = s32[1024]{0:T(1024)S(1)} all-reduce(s32[1024]{0:T(1024)S(1)} %bitcast_dynamic-update-slice_fusion), channel_id=3, replica_groups=mesh['dp'=2,'tensor'=8,'pipe'=2] {'dp','tensor'}, use_global_device_ids=true, to_apply=%add | all-reduce | flops 1024 | bytes 8192
  26.9 0.6 broadcast_subtract_fusion
  27.5 157.2 %all-gather.4.cloned.1.call-done = bf16[1,1024,7168]{2,1,0:T(8,128)(2,1)} async-done(((bf16[1,64,7168]{2,1,0:T(8,128)(2,1)}), bf16[1,1024,7168]{2,1,0:T(8,128)(2,1)}) %all-gather.4.cloned.1.call-update) | async-done | bytes 14680080 | tf_op jit(solution)/shard_map/all_gather | solution.py:16
  184.7 0.0 copy-start
  184.7 86.9 %fusion.3 = (f32[1024]{0:T(1024)S(1)}, f32[1024,5120]{1,0:T(8,128)}) fusion(bf16[5120,7168]{1,0:T(8,128)(2,1)} %param.4, bf16[1,1024,7168]{2,1,0:T(8,128)(2,1)} %all-gather.4.cloned.1.call-done), kind=kOutput, calls=%fused_computation.10 | convolution fusion | flops 75167170560 | bytes 109056000 | tf_op jit(solution)/shard_map/dot_general | solution.py:19
  271.7 38.8 %pmax.7 = f32[1024]{0:T(1024)S(1)} all-reduce(f32[1024]{0:T(1024)S(1)} %get-tuple-element.8), channel_id=1, replica_groups=mesh['dp'=2,'tensor'=8,'pipe'=2] {'dp','tensor'}, use_global_device_ids=true, to_apply=%region_1.2 | all-reduce | flops 1024 | bytes 8192 | tf_op jit(solution)/shard_map/pmax | solution.py:26
  310.5 0.0 copy-done
  310.5 10.1 %exponential_reduce_fusion = (f32[1024]{0:T(1024)S(1)}, f32[1024]{0:T(1024)S(1)}) fusion(f32[1024,5120]{1,0:T(8,128)} %get-tuple-element.9, f32[1024]{0:T(1024)S(1)} %pmax.7, s32[1024]{0:T(1024)S(1)} %copy-done), kind=kLoop, calls=%fused_computation.2 | loop fusion | flops 26212352 | bytes 20987904 | tf_op jit(solution)/shard_map/reduce_sum | solution.py:27
  320.6 37.1 %all-reduce.1 = (f32[1024]{0:T(1024)S(1)}, f32[1024]{0:T(1024)S(1)}) all-reduce(f32[1024]{0:T(1024)S(1)} %get-tuple-element.3, f32[1024]{0:T(1024)S(1)} %get-tuple-element.2), channel_id=1, replica_groups=mesh['dp'=2,'tensor'=8,'pipe'=2] {'dp','tensor'}, use_global_device_ids=true, to_apply=%region_5.6 | all-reduce | flops 2048 | bytes 16384 | tf_op jit(solution)/shard_map/psum | solution.py:28
  357.7 0.6 fusion.2
  358.3 3.1 psum.23
  361.4 0.6 dynamic-slice_bitcast_fusion
  (1 shorter events, 0.0 us)
Async XLA Ops:
  7.2 177.5 %all-gather.4.cloned.1.call-start = ((), (), s32[]{:S(2)}) async-start(), calls=%async_computation | async-start | bytes 15597568 | tf_op jit(solution)/shard_map/all_gather | solution.py:16
  184.7 125.8 %copy-start = (s32[1024]{0:T(1024)S(1)}, s32[1024]{0:T(1024)}, u32[]{:S(2)}) copy-start(s32[1024]{0:T(1024)} %broadcast_subtract_fusion) | copy-start | bytes 12292
Sparse Core Ops, SparseCore 0:
  10.7 173.9 all-gather.3
where the time goes:
time: 371 us
  waiting for transfers between devices  158 us (43%)
  blocking collectives  95.3 us (26%)
  matrix products  86.9 us (23%)
  between operations  16.5 us (4%)
  other arithmetic  11.3 us (3%)
    all_gather x1, waiting for transfers between devices, body(): lax.all_gather(tokens_own, ('dp', 'tensor'), axis=0, tiled=True)  157 us
    dot_general x1, matrix products, body(): lax.dot_general(gathered, head_table, (((1,), (1,)), ((), ())), preferred...  86.9 us
    pmax x1, blocking collectives, body(): maxima = lax.pmax(local_maxima, ('dp', 'tensor'))  38.8 us
    psum x1, blocking collectives, body(): totals, chosen = lax.psum((exp_sums, picked), ('dp', 'tensor'))  37.1 us
    unnamed x1, blocking collectives  16.3 us
    reduce_sum x1, other arithmetic, body(): exp_sums = jnp.sum(jnp.exp(logits - maxima[:, None]), axis=1)  10.1 us
  transfers between devices with their start and end apart: 1, of which 1 were waited for; matrix products, arithmetic and copies ran while one was open for 1% of the time, Pallas kernels for 0%

commit v1 on v0

--- a/solution.py
+++ b/solution.py
@@ -25,7 +25,7 @@
     local_maxima = jnp.max(logits, axis=1)
     maxima = lax.pmax(local_maxima, ("dp", "tensor"))
     exp_sums = jnp.sum(jnp.exp(logits - maxima[:, None]), axis=1)
-    totals, chosen = lax.psum((exp_sums, picked), ("dp", "tensor"))
+    totals, chosen = lax.psum(lax.psum((exp_sums, picked), "tensor"), "dp")
     losses = maxima + jnp.log(totals) - chosen
     own_losses = lax.dynamic_slice_in_dim(losses, position * own_count, own_count, 0)
     loss_sum = lax.psum(jnp.sum(losses), "pipe")

time: 371 us -> 356 us (0.960)
  blocking collectives: 95.3 us -> 80.6 us
    psum x1 -> x2, blocking collectives: 37.1 us -> 22.4 us  [body(): totals, chosen = lax.psum(lax.psum((exp_sums, picked), 'tensor'), 'dp')]
where the time goes in v1:
time: 356 us
  waiting for transfers between devices  158 us (44%)
  matrix products  86.9 us (24%)
  blocking collectives  80.6 us (23%)
  between operations  16.5 us (5%)
  other arithmetic  11.3 us (3%)
    all_gather x1, waiting for transfers between devices, body(): lax.all_gather(tokens_own, ('dp', 'tensor'), axis=0, tiled=True)  157 us
    dot_general x1, matrix products, body(): lax.dot_general(gathered, head_table, (((1,), (1,)), ((), ())), preferred...  86.9 us
    pmax x1, blocking collectives, body(): maxima = lax.pmax(local_maxima, ('dp', 'tensor'))  38.8 us
    psum x2, blocking collectives, body(): totals, chosen = lax.psum(lax.psum((exp_sums, picked), 'tensor'), 'dp')  22.4 us
    unnamed x1, blocking collectives  16.3 us
    reduce_sum x1, other arithmetic, body(): exp_sums = jnp.sum(jnp.exp(logits - maxima[:, None]), axis=1)  10.1 us
  transfers between devices with their start and end apart: 1, of which 1 were waited for; matrix products, arithmetic and copies ran while one was open for 1% of the time, Pallas kernels for 0%

profile of v1, /device:TPU:0, one launch (start us, length us, event | category | flops | bytes accessed | tf_op | source)
XLA Modules:
  0.0 355.9 jit_solution(15578580453674048867)
XLA Ops:
  7.2 0.0 all-gather.4.cloned.1.call-start
  7.2 0.7 all-gather.4.cloned.1.call-update
  7.9 1.2 dynamic-slice
  9.8 0.8 bitcast_dynamic-update-slice_fusion
  10.6 16.3 %all-reduce = s32[1024]{0:T(1024)S(1)} all-reduce(s32[1024]{0:T(1024)S(1)} %bitcast_dynamic-update-slice_fusion), channel_id=3, replica_groups=mesh['dp'=2,'tensor'=8,'pipe'=2] {'dp','tensor'}, use_global_device_ids=true, to_apply=%add | all-reduce | flops 1024 | bytes 8192
  26.9 0.6 broadcast_subtract_fusion
  27.5 157.2 %all-gather.4.cloned.1.call-done = bf16[1,1024,7168]{2,1,0:T(8,128)(2,1)} async-done(((bf16[1,64,7168]{2,1,0:T(8,128)(2,1)}), bf16[1,1024,7168]{2,1,0:T(8,128)(2,1)}) %all-gather.4.cloned.1.call-update) | async-done | bytes 14680080 | tf_op jit(solution)/shard_map/all_gather | solution.py:16
  184.7 0.0 copy-start
  184.7 86.9 %fusion.3 = (f32[1024]{0:T(1024)S(1)}, f32[1024,5120]{1,0:T(8,128)}) fusion(bf16[5120,7168]{1,0:T(8,128)(2,1)} %param.4, bf16[1,1024,7168]{2,1,0:T(8,128)(2,1)} %all-gather.4.cloned.1.call-done), kind=kOutput, calls=%fused_computation.10 | convolution fusion | flops 75167170560 | bytes 109056000 | tf_op jit(solution)/shard_map/dot_general | solution.py:19
  271.7 38.8 %pmax.7 = f32[1024]{0:T(1024)S(1)} all-reduce(f32[1024]{0:T(1024)S(1)} %get-tuple-element.10), channel_id=1, replica_groups=mesh['dp'=2,'tensor'=8,'pipe'=2] {'dp','tensor'}, use_global_device_ids=true, to_apply=%region_1.2 | all-reduce | flops 1024 | bytes 8192 | tf_op jit(solution)/shard_map/pmax | solution.py:26
  310.5 0.0 copy-done
  310.5 10.1 %exponential_reduce_fusion = (f32[1024]{0:T(1024)S(1)}, f32[1024]{0:T(1024)S(1)}) fusion(f32[1024,5120]{1,0:T(8,128)} %get-tuple-element.11, f32[1024]{0:T(1024)S(1)} %pmax.7, s32[1024]{0:T(1024)S(1)} %copy-done), kind=kLoop, calls=%fused_computation.2 | loop fusion | flops 26212352 | bytes 20987904 | tf_op jit(solution)/shard_map/reduce_sum | solution.py:27
  320.6 17.4 %all-reduce.1 = (f32[1024]{0:T(1024)S(1)}, f32[1024]{0:T(1024)S(1)}) all-reduce(f32[1024]{0:T(1024)S(1)} %get-tuple-element.3, f32[1024]{0:T(1024)S(1)} %get-tuple-element.2), channel_id=1, replica_groups=mesh['dp'=2,'tensor'=8,'pipe'=2] {'tensor'}, use_global_device_ids=true, to_apply=%region_6.7 | all-reduce | flops 2048 | bytes 16384 | tf_op jit(solution)/shard_map/psum | solution.py:28
  338.0 5.0 %all-reduce.2 = (f32[1024]{0:T(1024)S(1)}, f32[1024]{0:T(1024)S(1)}) all-reduce(f32[1024]{0:T(1024)S(1)} %get-tuple-element.4, f32[1024]{0:T(1024)S(1)} %get-tuple-element.5), channel_id=1, replica_groups=mesh['dp'=2,'tensor'=8,'pipe'=2] {'dp'}, use_global_device_ids=true, to_apply=%region_7.8 | all-reduce | flops 2048 | bytes 16384 | tf_op jit(solution)/shard_map/psum | solution.py:28
  343.0 0.6 fusion.2
  343.6 3.1 psum.39
  346.7 0.6 dynamic-slice_bitcast_fusion
  (1 shorter events, 0.0 us)
Async XLA Ops:
  7.2 177.5 %all-gather.4.cloned.1.call-start = ((), (), s32[]{:S(2)}) async-start(), calls=%async_computation | async-start | bytes 15597568 | tf_op jit(solution)/shard_map/all_gather | solution.py:16
  184.7 125.8 %copy-start = (s32[1024]{0:T(1024)S(1)}, s32[1024]{0:T(1024)}, u32[]{:S(2)}) copy-start(s32[1024]{0:T(1024)} %broadcast_subtract_fusion) | copy-start | bytes 12292
Sparse Core Ops, SparseCore 0:
  10.7 173.9 all-gather.3
